TPU v7x, 256 devices: a whole 4x4x8 slice. The times are simulated.
256 devices in a mesh: seq: 16 (over y, x), exp: 16 (over z, core).
Axes of the slice: x: 4, y: 4, z: 8, core: 2. Of those that a mesh axis runs over, the one named last changes fastest.
Arguments:
- x_in: bfloat16 [4096, 8192], P('seq', 'exp'), may hold values from -6 to 6
- z_gate: bfloat16 [4096, 8192], P('seq', 'exp'), may hold values from -6 to 6
- b_in: bfloat16 [4096, 128], P('seq'), may hold values from -0.52734375 to 0.52734375
- c_out: bfloat16 [4096, 128], P('seq'), may hold values from -0.1875 to 0.1875
- dt_step: float32 [4096, 128], P('seq', 'exp'), may hold values from 0.12 to 2052, as said below
- rate: float32 [128], P('exp'), may hold values from 0 to 0.06, as said below
- skip: float32 [128], P('exp'), may hold values from 0.5 to 1.5
- init_state: float32 [128, 64, 128], P('exp'), may hold values from -16.970562 to 16.970562
- residual: bfloat16 [4096, 8192], P(('seq', 'exp')), may hold values from -6 to 6
- norm_gain: float32 [8192], replicated, may hold values from 0.5 to 1.5
- expert_ids: int32 [4096, 2], P(('seq', 'exp')), may hold values from 0 to 15, all different within a row; in each aligned block of 16 rows (0 to 15, 16 to 31, ...) at most 3 rows name the same one
- gate_weights: float32 [4096, 2], P(('seq', 'exp')), may hold values from 0.2 to 1
- w_gate: bfloat16 [16, 8192, 2048], P('exp', None, 'seq'), may hold values from -0.0625 to 0.0625
- w_up: bfloat16 [16, 8192, 2048], P('exp', None, 'seq'), may hold values from -0.0625 to 0.0625
- w_down: bfloat16 [16, 2048, 8192], P('exp', 'seq'), may hold values from -0.125 to 0.125
Outputs:
- layer_out: bfloat16 [4096, 8192], P(('seq', 'exp'))
Inputs may be any that keep to these rules, and one draw needn't show every extreme that they name: `dt_step`: positive step sizes. `rate`: positive rates. `expert_ids`: each row names two different experts; among the rows of one device (aligned blocks of 16 rows) no expert is named by more than 3 rows, and in every draw some expert is named by exactly 3 rows of some block.
All inputs are finite; a program needn't handle non-finite values.
Results may differ from a plain program's by a relative error of at most 0.0095.
Values may be sent and summed in bfloat16 or wider, within the bound.
A program may use at most 128 MiB of HBM per device.

v0:
```python
import jax
import jax.numpy as jnp
from jax import lax
from jax.sharding import PartitionSpec as P

GROUP = 128
PRECISE = lax.Precision.HIGHEST


def entering_2(array, axis, combine, identity):
    devices, mine = (lax.axis_size(axis), lax.axis_index(axis))
    everything = jax.tree.map(
        lambda part, kind: lax.all_gather(part.astype(kind), axis),
        array,
        (jnp.bfloat16, jnp.bfloat16),
    )
    start = jax.tree.map(
        lambda part, zero: jnp.broadcast_to(jnp.asarray(zero, part.dtype), part.shape),
        array,
        identity,
    )

    def hop(k, before):
        reached = k < mine
        new = combine(
            before, jax.tree.map(lambda part, own: part[k].astype(own.dtype), everything, array)
        )
        return jax.tree.map(lambda a, b: jnp.where(reached, a, b), new, before)

    return lax.fori_loop(0, devices, hop, start)


def chain_combine(earlier, later):
    return (earlier[0] + later[0], jnp.exp(later[0])[:, None, None] * earlier[1] + later[1])


def on_device(
    x_in,
    z_gate,
    b_in,
    c_out,
    dt_step,
    rate,
    skip,
    init_state,
    residual,
    norm_gain,
    expert_ids,
    gate_weights,
    w_gate,
    w_up,
    w_down,
):
    token_count, channels = x_in.shape
    heads_here = rate.shape[0]
    head_width = channels // heads_here
    state_width = b_in.shape[1]
    blocks = token_count // GROUP
    inputs = x_in.astype(jnp.float32).reshape(blocks, GROUP, heads_here, head_width)
    keys_in = b_in.astype(jnp.float32).reshape(blocks, GROUP, state_width)
    queries = c_out.astype(jnp.float32).reshape(blocks, GROUP, state_width)
    log_steps = (-rate[None, :] * dt_step).reshape(blocks, GROUP, heads_here)
    cumulative = jnp.cumsum(log_steps, axis=1)
    scores = jnp.einsum("ctn,csn->cts", queries, keys_in, precision=PRECISE)
    causal = jnp.arange(GROUP)[:, None] >= jnp.arange(GROUP)[None, :]
    spread = cumulative[:, :, None, :] - cumulative[:, None, :, :]
    weights = jnp.exp(jnp.where(causal[None, :, :, None], spread, -jnp.inf)) * scores[..., None]
    intra_out = jnp.einsum("ctsh,cshp->cthp", weights, inputs, precision=PRECISE)
    tail_decay = jnp.exp(cumulative[:, -1:, :] - cumulative)
    block_state = jnp.einsum("csh,cshp,csn->chpn", tail_decay, inputs, keys_in, precision=PRECISE)
    block_log = cumulative[:, -1, :]

    def advance(carried, element):
        total_log, total_state = carried
        step_log, step_state = element
        updated = (
            total_log + step_log,
            jnp.exp(step_log)[:, None, None] * total_state + step_state,
        )
        return (updated, (total_log, total_state))

    zero_state = jnp.zeros((heads_here, head_width, state_width), jnp.float32)
    zero_log = jnp.zeros((heads_here,), jnp.float32)
    (device_log, device_state), (enter_log, enter_state) = lax.scan(
        advance, (zero_log, zero_state), (block_log, block_state)
    )
    prior_log, prior_state = entering_2(
        (device_log, device_state), "seq", chain_combine, (zero_log, zero_state)
    )
    incoming = prior_state + jnp.exp(prior_log)[:, None, None] * init_state
    entering = enter_state + jnp.exp(enter_log)[:, :, None, None] * incoming[None]
    inter_out = jnp.exp(cumulative)[..., None] * jnp.einsum(
        "chpn,ctn->cthp", entering, queries, precision=PRECISE
    )
    mixed_out = (intra_out + inter_out + skip[None, None, :, None] * inputs).reshape(
        token_count, channels
    )
    mixer = (mixed_out * jax.nn.silu(z_gate.astype(jnp.float32))).astype(jnp.bfloat16)
    token_mix = lax.all_to_all(mixer, "exp", split_axis=0, concat_axis=1, tiled=True)
    stream = (residual.astype(jnp.float32) + token_mix.astype(jnp.float32)).astype(jnp.bfloat16)
    widened = stream.astype(jnp.float32)
    normed = (
        widened
        * lax.rsqrt(jnp.mean(widened * widened, axis=-1, keepdims=True) + 1e-06)
        * norm_gain[None, :]
    ).astype(jnp.bfloat16)
    rows_here = residual.shape[0]
    owners = lax.axis_size("exp")
    local_experts = w_gate.shape[0]
    experts = owners * local_experts
    capacity = max(2, 2 * rows_here // experts + 1)
    width = residual.shape[1]
    chosen = expert_ids.reshape(-1)
    onehot = (chosen[:, None] == jnp.arange(experts)[None, :]).astype(jnp.int32)
    slot_index = jnp.sum((jnp.cumsum(onehot, axis=0) - onehot) * onehot, axis=1)
    target = chosen * capacity + slot_index
    placing = (target[None, :] == jnp.arange(experts * capacity)[:, None]).astype(jnp.bfloat16)
    pair_rows = jnp.repeat(normed, 2, axis=0)
    outgoing = jnp.dot(placing, pair_rows, preferred_element_type=jnp.float32).astype(jnp.bfloat16)
    outgoing = outgoing.reshape(owners, local_experts, 1, capacity, width)
    arrived = lax.all_to_all(outgoing, "exp", split_axis=0, concat_axis=2, tiled=True)
    segment = lax.all_gather(arrived, "seq", axis=1, tiled=True)
    flattened = segment.reshape(segment.shape[0], -1, segment.shape[-1])
    gate_proj = jnp.einsum("erd,edf->erf", flattened, w_gate, preferred_element_type=jnp.float32)
    up_proj = jnp.einsum("erd,edf->erf", flattened, w_up, preferred_element_type=jnp.float32)
    active = (jax.nn.silu(gate_proj) * up_proj).astype(jnp.bfloat16)
    partial_value = jnp.einsum("erf,efd->erd", active, w_down, preferred_element_type=jnp.float32)
    partials = partial_value.reshape(segment.shape[:-1] + (partial_value.shape[-1],))
    summed = lax.psum_scatter(partials.astype(jnp.bfloat16), "seq", scatter_dimension=1, tiled=True)
    returned = lax.all_to_all(summed, "exp", split_axis=2, concat_axis=0, tiled=True)
    results = returned.reshape(experts * capacity, width)
    picked = results[target].astype(jnp.float32).reshape(rows_here, 2, width)
    mixture = jnp.sum(picked * gate_weights[:, :, None], axis=1)
    return (widened + mixture).astype(jnp.bfloat16)


def solution(mesh):
    return jax.shard_map(
        on_device,
        mesh=mesh,
        in_specs=(
            P("seq", "exp"),
            P("seq", "exp"),
            P("seq", None),
            P("seq", None),
            P("seq", "exp"),
            P("exp"),
            P("exp"),
            P("exp", None, None),
            P(("seq", "exp"), None),
            P(),
            P(("seq", "exp"), None),
            P(("seq", "exp"), None),
            P("exp", None, "seq"),
            P("exp", None, "seq"),
            P("exp", "seq", None),
        ),
        out_specs=P(("seq", "exp"), None),
        check_vma=False,
    )
```

profile of v0, /device:TPU:1, one launch (start us, length us, event | category | flops | bytes accessed | tf_op | source)
XLA Modules:
  0.0 454.0 jit_solution(192723632810441709)
XLA Ops:
  8.6 1.3 reshape.209
  10.6 4.3 while.33
  11.5 1.3 dynamic_update_slice.14
  13.6 1.3 dynamic_update_slice.14
  16.3 1.3 dynamic-slice
  18.5 34.4 %all-reduce = bf16[128]{0:T(256)(128)(2,1)S(1)} all-reduce(bf16[128]{0:T(256)(128)(2,1)S(1)} %dynamic-update-slice), channel_id=2, replica_groups=mesh['seq'=16,'exp'=16] {'seq'}, use_global_device_ids=true, to_apply=%add | all-reduce | flops 128 | bytes 512
  53.7 1.1 copy.84
  55.2 13.5 %all-gather.6.cloned.1.call-done = bf16[128,64,128]{2,1,0:T(8,128)(2,1)} async-done(((bf16[8,64,128]{2,1,0:T(8,128)(2,1)}), bf16[128,64,128]{2,1,0:T(8,128)(2,1)}) %all-gather.6.cloned.1.call-update) | async-done | bytes 2097168 | tf_op jit(solution)/shard_map/all_gather | solution.py:13
  68.7 17.0 %while.34 = (s32[]{:T(128)}, f32[8]{0:T(128)S(1)}, f32[8,64,128]{2,1,0:T(8,128)S(1)}, s32[]{:T(128)}, bf16[16,8]{1,0:T(8,128)(2,1)S(1)}, /*index=5*/bf16[16,8,64,128]{3,2,1,0:T(8,128)(2,1)}, s32[]{:T(128)}, s32[]{:T(128)}) while((s32[]{:T(128)}, f32[8]{0:T(128)S(1)}, f32[8,64,128]{2,1,0:T(8,128)S(1)}, s32[]{:T(128)}, ...), condition=%wide.region_4.5_spmd.clone, body=%wide.region_3.4_spmd.clone.sunk | while | flops 327716 | bytes 655619 | solution.py:30
  85.7 1.0 multiply_add_fusion
  86.7 1.5 fusion.13
  88.2 1.3 fusion.12
  91.0 8.5 %all-to-all-start = ((bf16[16,16,512]{2,1,0:T(8,128)(2,1)}), bf16[16,16,512]{2,1,0:T(8,128)(2,1)S(1)}, u32[]{:S(2)}, u32[]{:S(2)}) async-start(bf16[16,16,512]{2,1,0:T(8,128)(2,1)} %bitcast.12), calls=%async_computation | async-start | bytes 524288 | tf_op jit(solution)/shard_map/all_to_all | solution.py:99
  99.9 11.3 %all-to-all-done = bf16[16,16,512]{2,1,0:T(8,128)(2,1)S(1)} async-done(((bf16[16,16,512]{2,1,0:T(8,128)(2,1)}), bf16[16,16,512]{2,1,0:T(8,128)(2,1)S(1)}, u32[]{:S(2)}, u32[]{:S(2)}) %all-to-all-start) | async-done | bytes 262176 | tf_op jit(solution)/shard_map/all_to_all | solution.py:99
  112.4 1.2 convolution_convert_fusion.1
  113.6 1.5 reshape.174
  115.1 31.2 %all_to_all.34 = bf16[16,1,1,3,8192]{4,3,2,1,0:T(4,128)(2,1)S(1)} all-to-all(bf16[16,1,1,3,8192]{4,3,2,1,0:T(4,128)(2,1)S(1)} %bitcast.114), channel_id=1, replica_groups=mesh['seq'=16,'exp'=16] {'exp'}, dimensions={0} | all-to-all | bytes 1572864 | tf_op jit(solution)/shard_map/all_to_all | solution.py:121
  146.3 1.5 copy.89
  148.0 89.6 %all-gather.8.cloned.1.call-done = bf16[256,1,1,3,8192]{4,0,3,2,1:T(8,128)(2,1)} async-done(((bf16[16,1,1,3,8192]{4,0,3,2,1:T(8,128)(2,1)}), bf16[256,1,1,3,8192]{4,0,3,2,1:T(8,128)(2,1)}) %all-gather.8.cloned.1.call-update) | async-done | bytes 12582928 | tf_op jit(solution)/shard_map/all_gather | solution.py:122
  237.6 18.8 %copy.90 = bf16[256,1,1,3,8192]{4,3,0,2,1:T(4,128)(2,1)} copy(bf16[256,1,1,3,8192]{4,0,3,2,1:T(8,128)(2,1)} %all-gather.8.cloned.1.call-done) | data formatting | bytes 25165824 | tf_op jit(solution)/shard_map/all_gather | solution.py:122
  256.4 26.2 %reshape.175 = bf16[768,8192]{1,0:T(8,128)(2,1)} reshape(bf16[256,1,1,3,8192]{4,3,0,2,1:T(4,128)(2,1)} %copy.90) | data formatting | bytes 25165824 | tf_op jit(solution)/shard_map/reshape.2
  282.7 7.7 %fusion.9 = f32[768,128]{1,0:T(8,128)S(1)} fusion(bf16[768,8192]{1,0:T(8,128)(2,1)} %reshape.175, bf16[1,8192,128]{2,1,0:T(8,128)(2,1)} %param.31), kind=kOutput, calls=%fused_computation.21 | convolution fusion | flops 1610612736 | bytes 15073280 | tf_op jit(solution)/shard_map/erd,edf->erf/dot_general | solution.py:124
  292.0 3.4 fusion.17
  295.6 6.4 %fusion.5 = bf16[1,16,16,3,8192]{4,2,3,1,0:T(8,128)(2,1)} fusion(bf16[1,128,8192]{2,1,0:T(8,128)(2,1)S(1)} %copy-done, bf16[16,16,3,128]{3,2,1,0:T(4,128)(2,1)S(1)} %dot_general.46), kind=kOutput, calls=%fused_computation.16 | convolution fusion | flops 1616904192 | bytes 14876672 | tf_op jit(solution)/shard_map/erf,efd->erd/dot_general | solution.py:127
  302.0 99.5 %reduce-scatter.7.cloned.1.call-done = bf16[1,1,16,3,8192]{4,2,3,1,0:T(8,128)(2,1)} async-done(((bf16[1,16,16,3,8192]{4,2,3,1,0:T(8,128)(2,1)}), bf16[1,1,16,3,8192]{4,2,3,1,0:T(8,128)(2,1)}) %reduce-scatter.7.cloned.1.call-update) | async-done | bytes 786448
  401.5 2.8 copy.92
  404.2 7.9 %all-to-all-start.2 = ((bf16[1,1,16,3,8192]{4,3,1,0,2:T(4,128)(2,1)}), bf16[1,1,16,3,8192]{4,3,1,0,2:T(4,128)(2,1)}, u32[]{:S(2)}, u32[]{:S(2)}) async-start(bf16[1,1,16,3,8192]{4,3,1,0,2:T(4,128)(2,1)} %copy.92), calls=%async_computation.2 | async-start | bytes 2097152 | tf_op jit(solution)/shard_map/all_to_all | solution.py:130
  412.4 27.8 %all-to-all-done.2 = bf16[1,1,16,3,8192]{4,3,1,0,2:T(4,128)(2,1)} async-done(((bf16[1,1,16,3,8192]{4,3,1,0,2:T(4,128)(2,1)}), bf16[1,1,16,3,8192]{4,3,1,0,2:T(4,128)(2,1)}, u32[]{:S(2)}, u32[]{:S(2)}) %all-to-all-start.2) | async-done | bytes 786464 | tf_op jit(solution)/shard_map/all_to_all | solution.py:130
  440.2 1.7 reshape.179
  441.9 1.7 gather_fusion
  443.6 1.7 reshape.183
  445.3 1.4 multiply_reduce_fusion
  (116 shorter events, 29.6 us)
Async XLA Ops:
  6.5 289.0 %copy-start = (bf16[1,128,8192]{2,1,0:T(8,128)(2,1)S(1)}, bf16[1,128,8192]{2,1,0:T(8,128)(2,1)}, u32[]{:S(2)}) copy-start(bf16[1,128,8192]{2,1,0:T(8,128)(2,1)} %param.33) | copy-start | bytes 6291460
  6.5 3.7 copy-start.4
  6.5 62.1 %all-gather.6.cloned.1.call-start = ((), (), s32[]{:S(2)}) async-start(), calls=%async_computation.4 | async-start | bytes 2228224 | tf_op jit(solution)/shard_map/all_gather | solution.py:13
  10.6 44.2 %copy-start.7 = (s32[16,2]{0,1:T(2,128)S(1)}, s32[16,2]{0,1:T(2,128)}, u32[]{:S(2)}) copy-start(s32[16,2]{0,1:T(2,128)} %param.29) | copy-start | bytes 388
  10.6 44.4 %copy-start.2 = (bf16[256,128]{1,0:T(8,128)(2,1)S(1)}, bf16[256,128]{1,0:T(8,128)(2,1)}, u32[]{:S(2)}) copy-start(bf16[256,128]{1,0:T(8,128)(2,1)} %param.22) | copy-start | bytes 196612
  68.7 19.5 %copy-start.6 = (f32[2,128,8]{1,2,0:T(8,128)S(1)}, f32[2,128,8]{1,2,0:T(8,128)}, u32[]{:S(2)}) copy-start(f32[2,128,8]{1,2,0:T(8,128)} %copy.76) | copy-start | bytes 24580
  68.7 19.5 %copy-start.10 = (f32[8]{0:T(128)S(1)}, f32[8]{0:T(128)}, u32[]{:S(2)}) copy-start(f32[8]{0:T(128)} %param.25) | copy-start | bytes 100
  90.0 21.4 %copy-start.3 = (bf16[16,8192]{1,0:T(8,128)(2,1)S(1)}, bf16[16,8192]{1,0:T(8,128)(2,1)}, u32[]{:S(2)}) copy-start(bf16[16,8192]{1,0:T(8,128)(2,1)} %param.27) | copy-start | bytes 786436
  90.2 21.4 %copy-start.5 = (f32[8192]{0:T(1024)S(1)}, f32[8192]{0:T(1024)}, u32[]{:S(2)}) copy-start(f32[8192]{0:T(1024)} %param.28) | copy-start | bytes 98308
  91.0 20.2 %all-to-all-start = ((bf16[16,16,512]{2,1,0:T(8,128)(2,1)}), bf16[16,16,512]{2,1,0:T(8,128)(2,1)S(1)}, u32[]{:S(2)}, u32[]{:S(2)}) async-start(bf16[16,16,512]{2,1,0:T(8,128)(2,1)} %bitcast.12), calls=%async_computation | async-start | bytes 524288 | tf_op jit(solution)/shard_map/all_to_all | solution.py:99
  99.6 138.0 %all-gather.8.cloned.1.call-start = ((), (), s32[]{:S(2)}) async-start(), calls=%async_computation.5 | async-start | bytes 13369344 | tf_op jit(solution)/shard_map/all_gather | solution.py:122
  147.8 253.7 %reduce-scatter.7.cloned.1.call-start = ((), (), s32[]{:S(2)}) async-start(), calls=%async_computation.6 | async-start | bytes 13369344
  282.7 8.8 %copy-start.1 = (bf16[768,8192]{1,0:T(8,128)(2,1)S(1)}, bf16[768,8192]{1,0:T(8,128)(2,1)}, u32[]{:S(2)}) copy-start(bf16[768,8192]{1,0:T(8,128)(2,1)} %reshape.175) | copy-start | bytes 37748740
  282.7 9.4 %copy-start.9 = (bf16[1,8192,128]{2,1,0:T(8,128)(2,1)S(1)}, bf16[1,8192,128]{2,1,0:T(8,128)(2,1)}, u32[]{:S(2)}) copy-start(bf16[1,8192,128]{2,1,0:T(8,128)(2,1)} %param.32) | copy-start | bytes 6291460
  302.0 110.4 %copy-start.8 = (f32[16,2]{0,1:T(2,128)S(1)}, f32[16,2]{0,1:T(2,128)}, u32[]{:S(2)}) copy-start(f32[16,2]{0,1:T(2,128)} %param.30) | copy-start | bytes 388
  404.2 35.9 %all-to-all-start.2 = ((bf16[1,1,16,3,8192]{4,3,1,0,2:T(4,128)(2,1)}), bf16[1,1,16,3,8192]{4,3,1,0,2:T(4,128)(2,1)}, u32[]{:S(2)}, u32[]{:S(2)}) async-start(bf16[1,1,16,3,8192]{4,3,1,0,2:T(4,128)(2,1)} %copy.92), calls=%async_computation.2 | async-start | bytes 2097152 | tf_op jit(solution)/shard_map/all_to_all | solution.py:130
Sparse Core Ops, SparseCore 0:
  15.7 52.9 all-gather.5
  147.9 89.6 all-gather.7
  302.1 99.3 reduce-scatter.6
where the time goes:
time: 456 us; the launch traced here: 454 us
  waiting for transfers between devices  242 us (53%)
  local copies, waits for them, and re-layouts  68.5 us (15%)
  blocking collectives  65.6 us (14%)
  other arithmetic  24.9 us (5%)
  matrix products  22.1 us (5%)
  starting transfers between devices  16.7 us (4%)
  between operations  14.1 us (3%)
    unnamed x4, waiting for transfers between devices  99.5 us
    all_gather x1, waiting for transfers between devices, on_device(): segment = lax.all_gather(arrived, 'seq', axis=1, tiled=True)  89.6 us
    unnamed x1, blocking collectives  34.4 us
    all_to_all x1, blocking collectives, on_device(): lax.all_to_all(outgoing, 'exp', split_axis=0, concat_axis=2, tiled=True)  31.2 us
    all_to_all x1, waiting for transfers between devices, on_device(): lax.all_to_all(summed, 'exp', split_axis=2, concat_axis=0, tiled=True)  27.8 us
    another operation x1, local copies, waits for them, and re-layouts  26.2 us
    all_gather x1, local copies, waits for them, and re-layouts, on_device(): segment = lax.all_gather(arrived, 'seq', axis=1, tiled=True)  18.8 us
    select_n x16, other arithmetic, hop(): return jax.tree.map(lambda a, b: jnp.where(reached, a, b), new, before)  16.2 us
  transfers between devices with their start and end apart: 5, of which 5 were waited for; matrix products, arithmetic and copies ran while one was open for 1% of the time, Pallas kernels for 0%

commit v1 on v0

--- a/solution.py
+++ b/solution.py
@@ -5,6 +5,19 @@
 
 GROUP = 128
 PRECISE = lax.Precision.HIGHEST
+
+
+def collect(array, axis, dim):
+    ways = lax.axis_size(axis)
+    up = [(d, (d + 1) % ways) for d in range(ways)]
+    down = [(d, (d - 1) % ways) for d in range(ways)]
+    earlier, later = ([array], [array])
+    for _ in range(ways // 2):
+        earlier.append(lax.ppermute(earlier[-1], axis, up))
+    for _ in range((ways - 1) // 2):
+        later.append(lax.ppermute(later[-1], axis, down))
+    line = jnp.concatenate([*earlier[::-1], *later[1:]], axis=dim)
+    return jnp.roll(line, (lax.axis_index(axis) - ways // 2) * array.shape[dim], axis=dim)
 
 
 def entering_2(array, axis, combine, identity):
@@ -119,7 +132,7 @@
     outgoing = jnp.dot(placing, pair_rows, preferred_element_type=jnp.float32).astype(jnp.bfloat16)
     outgoing = outgoing.reshape(owners, local_experts, 1, capacity, width)
     arrived = lax.all_to_all(outgoing, "exp", split_axis=0, concat_axis=2, tiled=True)
-    segment = lax.all_gather(arrived, "seq", axis=1, tiled=True)
+    segment = collect(arrived, "seq", 1)
     flattened = segment.reshape(segment.shape[0], -1, segment.shape[-1])
     gate_proj = jnp.einsum("erd,edf->erf", flattened, w_gate, preferred_element_type=jnp.float32)
     up_proj = jnp.einsum("erd,edf->erf", flattened, w_up, preferred_element_type=jnp.float32)

time: 456 us -> 603 us (1.32); the launches traced: 454 us -> 592 us
  local copies, waits for them, and re-layouts: 68.5 us -> 133 us
  starting transfers between devices: 16.7 us -> 54 us
  waiting for transfers between devices: 242 us -> 268 us
  matrix products: 22.1 us -> 29.1 us
    ppermute x0 -> x15, waiting for transfers between devices: none -> 120 us  [the longest x8 120 us: collect(): earlier.append(lax.ppermute(earlier[-1], axis, up))]
    all_gather x1 -> x0, waiting for transfers between devices: 89.6 us -> none  [on_device(): segment = lax.all_gather(arrived, 'seq', axis=1, tiled=True)]
    unnamed x28 -> x83, local copies, waits for them, and re-layouts: 4.48 us -> 78.4 us
    ppermute x0 -> x15, starting transfers between devices: none -> 37.4 us  [the longest x7 36.6 us: collect(): later.append(lax.ppermute(later[-1], axis, down))]
    all_gather x1 -> x0, local copies, waits for them, and re-layouts: 18.8 us -> none  [on_device(): segment = lax.all_gather(arrived, 'seq', axis=1, tiled=True)]
    dynamic_slice x0 -> x1, local copies, waits for them, and re-layouts: none -> 12.1 us  [collect(): jnp.roll(line, (lax.axis_index(axis) - ways // 2) * array.shape[dim], axi...]
    unnamed x4 -> x3, waiting for transfers between devices: 99.5 us -> 96.2 us
  transfers between devices with their start and end apart: 5 -> 19, of which waited for: 5 -> 13; matrix products, arithmetic and copies ran while one was open for 1% -> 8% of each run, Pallas kernels for 0% -> 0%
where the time goes in v1:
time: 603 us; the launch traced here: 592 us
  waiting for transfers between devices  268 us (44%)
  local copies, waits for them, and re-layouts  133 us (22%)
  blocking collectives  65.8 us (11%)
  starting transfers between devices  54 us (9%)
  matrix products  29.1 us (5%)
  other arithmetic  26.6 us (4%)
  between operations  14.7 us (2%)
    ppermute x8, waiting for transfers between devices, collect(): earlier.append(lax.ppermute(earlier[-1], axis, up))  120 us
    unnamed x3, waiting for transfers between devices  96.2 us
    unnamed x83, local copies, waits for them, and re-layouts  78.4 us
    ppermute x7, starting transfers between devices, collect(): later.append(lax.ppermute(later[-1], axis, down))  36.6 us
    unnamed x1, blocking collectives  34.3 us
    all_to_all x1, blocking collectives, on_device(): lax.all_to_all(outgoing, 'exp', split_axis=0, concat_axis=2, tiled=True)  31.5 us
    all_to_all x1, waiting for transfers between devices, on_device(): lax.all_to_all(summed, 'exp', split_axis=2, concat_axis=0, tiled=True)  27.7 us
    another operation x1, local copies, waits for them, and re-layouts  26.3 us
  transfers between devices with their start and end apart: 19, of which 13 were waited for; matrix products, arithmetic and copies ran while one was open for 8% of the time, Pallas kernels for 0%

profile of v1, /device:TPU:1, one launch (start us, length us, event | category | flops | bytes accessed | tf_op | source)
XLA Modules:
  0.0 592.2 jit_solution(738378900589573819)
XLA Ops:
  16.3 34.3 %all-reduce = bf16[128]{0:T(256)(128)(2,1)S(1)} all-reduce(bf16[128]{0:T(256)(128)(2,1)S(1)} %dynamic-update-slice), channel_id=2, replica_groups=mesh['seq'=16,'exp'=16] {'seq'}, use_global_device_ids=true, to_apply=%add | all-reduce | flops 128 | bytes 512
  53.9 13.1 %all-gather.4.cloned.1.call-done = bf16[128,64,128]{2,1,0:T(8,128)(2,1)} async-done(((bf16[8,64,128]{2,1,0:T(8,128)(2,1)}), bf16[128,64,128]{2,1,0:T(8,128)(2,1)}) %all-gather.4.cloned.1.call-update) | async-done | bytes 2097168 | tf_op jit(solution)/shard_map/all_gather | solution.py:26
  67.0 16.9 %while.34 = (s32[]{:T(128)}, f32[8]{0:T(128)S(1)}, f32[8,64,128]{2,1,0:T(8,128)S(1)}, s32[]{:T(128)}, bf16[16,8]{1,0:T(8,128)(2,1)S(1)}, /*index=5*/bf16[16,8,64,128]{3,2,1,0:T(8,128)(2,1)}, s32[]{:T(128)}, s32[]{:T(128)}) while((s32[]{:T(128)}, f32[8]{0:T(128)S(1)}, f32[8,64,128]{2,1,0:T(8,128)S(1)}, s32[]{:T(128)}, ...), condition=%wide.region_4.5_spmd.clone, body=%wide.region_3.4_spmd.clone.sunk | while | flops 327716 | bytes 655619 | solution.py:43
  89.9 8.7 %all-to-all-start = ((bf16[16,16,512]{2,1,0:T(8,128)(2,1)}), bf16[16,16,512]{2,1,0:T(8,128)(2,1)S(1)}, u32[]{:S(2)}, u32[]{:S(2)}) async-start(bf16[16,16,512]{2,1,0:T(8,128)(2,1)} %bitcast.12), calls=%async_computation | async-start | bytes 524288 | tf_op jit(solution)/shard_map/all_to_all | solution.py:112
  99.0 11.3 %all-to-all-done = bf16[16,16,512]{2,1,0:T(8,128)(2,1)S(1)} async-done(((bf16[16,16,512]{2,1,0:T(8,128)(2,1)}), bf16[16,16,512]{2,1,0:T(8,128)(2,1)S(1)}, u32[]{:S(2)}, u32[]{:S(2)}) %all-to-all-start) | async-done | bytes 262176 | tf_op jit(solution)/shard_map/all_to_all | solution.py:112
  116.6 31.5 %all_to_all.34 = bf16[16,1,1,3,8192]{4,3,2,1,0:T(4,128)(2,1)S(1)} all-to-all(bf16[16,1,1,3,8192]{4,3,2,1,0:T(4,128)(2,1)} %bitcast.116), channel_id=1, replica_groups=mesh['seq'=16,'exp'=16] {'exp'}, dimensions={0} | all-to-all | bytes 1572864 | tf_op jit(solution)/shard_map/all_to_all | solution.py:134
  149.5 21.3 %collective-permute-done = bf16[1,1,16,3,8192]{4,2,3,1,0:T(8,128)(2,1)S(1)} collective-permute-done((bf16[1,1,16,3,8192]{4,2,3,1,0:T(8,128)(2,1)S(1)}, bf16[1,1,16,3,8192]{4,2,3,1,0:T(8,128)(2,1)S(1)}, u32[]{:S(2)}, u32[]{:S(2)}) %collective-permute-start) | collective-permute-done | bytes 786464 | tf_op jit(solution)/shard_map/ppermute | solution.py:16
  171.7 4.8 collective-permute-start.8
  176.5 17.5 %collective-permute-done.1 = bf16[1,1,16,3,8192]{4,2,3,1,0:T(8,128)(2,1)S(1)} collective-permute-done((bf16[1,1,16,3,8192]{4,2,3,1,0:T(8,128)(2,1)S(1)}, bf16[1,1,16,3,8192]{4,2,3,1,0:T(8,128)(2,1)S(1)}, u32[]{:S(2)}, u32[]{:S(2)}) %collective-permute-start.1) | collective-permute-done | bytes 786464 | tf_op jit(solution)/shard_map/ppermute | solution.py:16
  194.9 4.8 collective-permute-start.9
  199.7 15.7 %collective-permute-done.2 = bf16[1,1,16,3,8192]{4,2,3,1,0:T(8,128)(2,1)S(1)} collective-permute-done((bf16[1,1,16,3,8192]{4,2,3,1,0:T(8,128)(2,1)S(1)}, bf16[1,1,16,3,8192]{4,2,3,1,0:T(8,128)(2,1)S(1)}, u32[]{:S(2)}, u32[]{:S(2)}) %collective-permute-start.2) | collective-permute-done | bytes 786464 | tf_op jit(solution)/shard_map/ppermute | solution.py:16
  215.4 5.5 collective-permute-start.10
  220.9 14.9 %collective-permute-done.3 = bf16[1,1,16,3,8192]{4,2,3,1,0:T(8,128)(2,1)S(1)} collective-permute-done((bf16[1,1,16,3,8192]{4,2,3,1,0:T(8,128)(2,1)S(1)}, bf16[1,1,16,3,8192]{4,2,3,1,0:T(8,128)(2,1)S(1)}, u32[]{:S(2)}, u32[]{:S(2)}) %collective-permute-start.3) | collective-permute-done | bytes 786464 | tf_op jit(solution)/shard_map/ppermute | solution.py:16
  235.8 5.2 collective-permute-start.11
  241.1 14.2 %collective-permute-done.4 = bf16[1,1,16,3,8192]{4,2,3,1,0:T(8,128)(2,1)S(1)} collective-permute-done((bf16[1,1,16,3,8192]{4,2,3,1,0:T(8,128)(2,1)S(1)}, bf16[1,1,16,3,8192]{4,2,3,1,0:T(8,128)(2,1)S(1)}, u32[]{:S(2)}, u32[]{:S(2)}) %collective-permute-start.4) | collective-permute-done | bytes 786464 | tf_op jit(solution)/shard_map/ppermute | solution.py:16
  256.2 5.0 collective-permute-start.12
  261.2 12.7 %collective-permute-done.5 = bf16[1,1,16,3,8192]{4,2,3,1,0:T(8,128)(2,1)S(1)} collective-permute-done((bf16[1,1,16,3,8192]{4,2,3,1,0:T(8,128)(2,1)S(1)}, bf16[1,1,16,3,8192]{4,2,3,1,0:T(8,128)(2,1)S(1)}, u32[]{:S(2)}, u32[]{:S(2)}) %collective-permute-start.5) | collective-permute-done | bytes 786464 | tf_op jit(solution)/shard_map/ppermute | solution.py:16
  273.9 5.6 collective-permute-start.13
  279.6 12.1 %collective-permute-done.6 = bf16[1,1,16,3,8192]{4,2,3,1,0:T(8,128)(2,1)} collective-permute-done((bf16[1,1,16,3,8192]{4,2,3,1,0:T(8,128)(2,1)S(1)}, bf16[1,1,16,3,8192]{4,2,3,1,0:T(8,128)(2,1)}, u32[]{:S(2)}, u32[]{:S(2)}) %collective-permute-start.6) | collective-permute-done | bytes 786464 | tf_op jit(solution)/shard_map/ppermute | solution.py:16
  291.8 5.7 collective-permute-start.14
  297.5 11.3 %collective-permute-done.7 = bf16[1,1,16,3,8192]{4,2,3,1,0:T(8,128)(2,1)} collective-permute-done((bf16[1,1,16,3,8192]{4,2,3,1,0:T(8,128)(2,1)}, bf16[1,1,16,3,8192]{4,2,3,1,0:T(8,128)(2,1)}, u32[]{:S(2)}, u32[]{:S(2)}) %collective-permute-start.7) | collective-permute-done | bytes 786464 | tf_op jit(solution)/shard_map/ppermute | solution.py:16
  319.9 2.8 copy_dynamic-update-slice_fusion.20
  328.3 2.9 copy_dynamic-update-slice_fusion.14
  353.9 3.2 copy_dynamic-update-slice_fusion.27
  382.6 12.1 %constant_dynamic-slice_fusion.2 = bf16[1,16,16,3,8192]{4,3,2,1,0:T(4,128)(2,1)} fusion(bf16[1,32,16,3,8192]{4,3,2,1,0:T(4,128)(2,1)} %copy_dynamic-update-slice_fusion.1, s32[]{:T(128)S(6)} %select_n.67), kind=kLoop, calls=%fused_computation.113 | loop fusion | bytes 25165828 | tf_op jit(solution)/shard_map/jit(_roll_dynamic)/dynamic_slice | solution.py:20
  394.6 26.3 %reshape.175 = bf16[768,8192]{1,0:T(8,128)(2,1)} reshape(bf16[1,16,16,3,8192]{4,3,2,1,0:T(4,128)(2,1)} %constant_dynamic-slice_fusion.2) | data formatting | bytes 25165824 | tf_op jit(solution)/shard_map/reshape.3
  420.9 7.0 %fusion.9 = f32[768,128]{1,0:T(8,128)S(1)} fusion(bf16[768,8192]{1,0:T(8,128)(2,1)} %reshape.175, bf16[1,8192,128]{2,1,0:T(8,128)(2,1)} %param.31), kind=kOutput, calls=%fused_computation.21 | convolution fusion | flops 1610612736 | bytes 15073280 | tf_op jit(solution)/shard_map/erd,edf->erf/dot_general | solution.py:137
  428.0 8.6 %fusion.17 = bf16[768,128]{1,0:T(8,128)(2,1)S(1)} fusion(bf16[768,8192]{1,0:T(8,128)(2,1)} %reshape.175, bf16[1,8192,128]{2,1,0:T(8,128)(2,1)} %param.32, f32[768,128]{1,0:T(8,128)S(1)} %fusion.9), kind=kOutput, calls=%fused_computation.29 | convolution fusion | flops 1611202560 | bytes 15269888 | tf_op jit(solution)/shard_map/erd,edf->erf/dot_general | solution.py:138
  436.6 6.3 %fusion.5 = bf16[1,16,16,3,8192]{4,2,3,1,0:T(8,128)(2,1)} fusion(bf16[1,128,8192]{2,1,0:T(8,128)(2,1)S(1)} %copy-done, bf16[16,16,3,128]{3,2,1,0:T(4,128)(2,1)S(1)} %dot_general.46), kind=kOutput, calls=%fused_computation.16 | convolution fusion | flops 1616904192 | bytes 14876672 | tf_op jit(solution)/shard_map/erf,efd->erd/dot_general | solution.py:140
  443.0 96.2 %reduce-scatter.7.cloned.1.call-done = bf16[1,1,16,3,8192]{4,2,3,1,0:T(8,128)(2,1)} async-done(((bf16[1,16,16,3,8192]{4,2,3,1,0:T(8,128)(2,1)}), bf16[1,1,16,3,8192]{4,2,3,1,0:T(8,128)(2,1)}) %reduce-scatter.7.cloned.1.call-update) | async-done | bytes 786448
  542.0 7.9 %all-to-all-start.2 = ((bf16[1,1,16,3,8192]{4,3,1,0,2:T(4,128)(2,1)}), bf16[1,1,16,3,8192]{4,3,1,0,2:T(4,128)(2,1)}, u32[]{:S(2)}, u32[]{:S(2)}) async-start(bf16[1,1,16,3,8192]{4,3,1,0,2:T(4,128)(2,1)} %copy.122), calls=%async_computation.2 | async-start | bytes 2097152 | tf_op jit(solution)/shard_map/all_to_all | solution.py:143
  550.2 27.7 %all-to-all-done.2 = bf16[1,1,16,3,8192]{4,3,1,0,2:T(4,128)(2,1)} async-done(((bf16[1,1,16,3,8192]{4,3,1,0,2:T(4,128)(2,1)}), bf16[1,1,16,3,8192]{4,3,1,0,2:T(4,128)(2,1)}, u32[]{:S(2)}, u32[]{:S(2)}) %all-to-all-start.2) | async-done | bytes 786464 | tf_op jit(solution)/shard_map/all_to_all | solution.py:143
  (199 shorter events, 122.6 us)
Async XLA Ops:
  6.5 430.1 %copy-start = (bf16[1,128,8192]{2,1,0:T(8,128)(2,1)S(1)}, bf16[1,128,8192]{2,1,0:T(8,128)(2,1)}, u32[]{:S(2)}) copy-start(bf16[1,128,8192]{2,1,0:T(8,128)(2,1)} %param.33) | copy-start | bytes 6291460
  6.5 60.5 %all-gather.4.cloned.1.call-start = ((), (), s32[]{:S(2)}) async-start(), calls=%async_computation.4 | async-start | bytes 2228224 | tf_op jit(solution)/shard_map/all_gather | solution.py:26
  89.9 20.4 %all-to-all-start = ((bf16[16,16,512]{2,1,0:T(8,128)(2,1)}), bf16[16,16,512]{2,1,0:T(8,128)(2,1)S(1)}, u32[]{:S(2)}, u32[]{:S(2)}) async-start(bf16[16,16,512]{2,1,0:T(8,128)(2,1)} %bitcast.12), calls=%async_computation | async-start | bytes 524288 | tf_op jit(solution)/shard_map/all_to_all | solution.py:112
  98.7 440.6 %reduce-scatter.7.cloned.1.call-start = ((), (), s32[]{:S(2)}) async-start(), calls=%async_computation.5 | async-start | bytes 13369344
  148.7 22.1 %collective-permute-start = (bf16[1,1,16,3,8192]{4,2,3,1,0:T(8,128)(2,1)S(1)}, bf16[1,1,16,3,8192]{4,2,3,1,0:T(8,128)(2,1)S(1)}, u32[]{:S(2)}, u32[]{:S(2)}) collective-permute-start(bf16[1,1,16,3,8192]{4,2,3,1,0:T(8,128)(2,1)S(1)} %copy.89), channel_id=1, source_target_pairs={{0,16},{16,32},{32,48},{48,64},{64,80},{80,96},{96,112},{112,128},... | collective-permute-start | bytes 2359304 | tf_op jit(solution)/shard_map/ppermute | solution.py:16
  171.7 22.3 %collective-permute-start.1 = (bf16[1,1,16,3,8192]{4,2,3,1,0:T(8,128)(2,1)S(1)}, bf16[1,1,16,3,8192]{4,2,3,1,0:T(8,128)(2,1)S(1)}, u32[]{:S(2)}, u32[]{:S(2)}) collective-permute-start(bf16[1,1,16,3,8192]{4,2,3,1,0:T(8,128)(2,1)S(1)} %collective-permute-done), channel_id=1, source_target_pairs={{0,16},{16,32},{32,48},{48,64},{64,80},{80,96},{96,112},{112,128},... | collective-permute-start | bytes 2359304 | tf_op jit(solution)/shard_map/ppermute | solution.py:16
  171.7 22.3 %collective-permute-start.8 = (bf16[1,1,16,3,8192]{4,2,3,1,0:T(8,128)(2,1)S(1)}, bf16[1,1,16,3,8192]{4,2,3,1,0:T(8,128)(2,1)S(1)}, u32[]{:S(2)}, u32[]{:S(2)}) collective-permute-start(bf16[1,1,16,3,8192]{4,2,3,1,0:T(8,128)(2,1)S(1)} %copy.89), channel_id=1, source_target_pairs={{0,240},{16,0},{32,16},{48,32},{64,48},{80,64},{96,80},{112,96},{1... | collective-permute-start | bytes 2359304 | tf_op jit(solution)/shard_map/ppermute | solution.py:18
  194.0 21.4 %collective-permute-start.2 = (bf16[1,1,16,3,8192]{4,2,3,1,0:T(8,128)(2,1)S(1)}, bf16[1,1,16,3,8192]{4,2,3,1,0:T(8,128)(2,1)S(1)}, u32[]{:S(2)}, u32[]{:S(2)}) collective-permute-start(bf16[1,1,16,3,8192]{4,2,3,1,0:T(8,128)(2,1)S(1)} %collective-permute-done.1), channel_id=1, source_target_pairs={{0,16},{16,32},{32,48},{48,64},{64,80},{80,96},{96,112},{112,128},... | collective-permute-start | bytes 2359304 | tf_op jit(solution)/shard_map/ppermute | solution.py:16
  194.9 20.4 %collective-permute-start.9 = (bf16[1,1,16,3,8192]{4,2,3,1,0:T(8,128)(2,1)S(1)}, bf16[1,1,16,3,8192]{4,2,3,1,0:T(8,128)(2,1)S(1)}, u32[]{:S(2)}, u32[]{:S(2)}) collective-permute-start(bf16[1,1,16,3,8192]{4,2,3,1,0:T(8,128)(2,1)S(1)} %collective-permute-done.8), channel_id=1, source_target_pairs={{0,240},{16,0},{32,16},{48,32},{64,48},{80,64},{96,80},{112,96},{1... | collective-permute-start | bytes 2359304 | tf_op jit(solution)/shard_map/ppermute | solution.py:18
  215.3 20.4 %collective-permute-start.3 = (bf16[1,1,16,3,8192]{4,2,3,1,0:T(8,128)(2,1)S(1)}, bf16[1,1,16,3,8192]{4,2,3,1,0:T(8,128)(2,1)S(1)}, u32[]{:S(2)}, u32[]{:S(2)}) collective-permute-start(bf16[1,1,16,3,8192]{4,2,3,1,0:T(8,128)(2,1)S(1)} %collective-permute-done.2), channel_id=1, source_target_pairs={{0,16},{16,32},{32,48},{48,64},{64,80},{80,96},{96,112},{112,128},... | collective-permute-start | bytes 2359304 | tf_op jit(solution)/shard_map/ppermute | solution.py:16
  215.4 20.4 %collective-permute-start.10 = (bf16[1,1,16,3,8192]{4,2,3,1,0:T(8,128)(2,1)S(1)}, bf16[1,1,16,3,8192]{4,2,3,1,0:T(8,128)(2,1)S(1)}, u32[]{:S(2)}, u32[]{:S(2)}) collective-permute-start(bf16[1,1,16,3,8192]{4,2,3,1,0:T(8,128)(2,1)S(1)} %collective-permute-done.9), channel_id=1, source_target_pairs={{0,240},{16,0},{32,16},{48,32},{64,48},{80,64},{96,80},{112,96},{1... | collective-permute-start | bytes 2359304 | tf_op jit(solution)/shard_map/ppermute | solution.py:18
  235.8 19.5 %collective-permute-start.4 = (bf16[1,1,16,3,8192]{4,2,3,1,0:T(8,128)(2,1)S(1)}, bf16[1,1,16,3,8192]{4,2,3,1,0:T(8,128)(2,1)S(1)}, u32[]{:S(2)}, u32[]{:S(2)}) collective-permute-start(bf16[1,1,16,3,8192]{4,2,3,1,0:T(8,128)(2,1)S(1)} %collective-permute-done.3), channel_id=1, source_target_pairs={{0,16},{16,32},{32,48},{48,64},{64,80},{80,96},{96,112},{112,128},... | collective-permute-start | bytes 2359304 | tf_op jit(solution)/shard_map/ppermute | solution.py:16
  235.8 19.5 %collective-permute-start.11 = (bf16[1,1,16,3,8192]{4,2,3,1,0:T(8,128)(2,1)S(1)}, bf16[1,1,16,3,8192]{4,2,3,1,0:T(8,128)(2,1)S(1)}, u32[]{:S(2)}, u32[]{:S(2)}) collective-permute-start(bf16[1,1,16,3,8192]{4,2,3,1,0:T(8,128)(2,1)S(1)} %collective-permute-done.10), channel_id=1, source_target_pairs={{0,240},{16,0},{32,16},{48,32},{64,48},{80,64},{96,80},{112,96},{1... | collective-permute-start | bytes 2359304 | tf_op jit(solution)/shard_map/ppermute | solution.py:18
  255.3 18.6 %collective-permute-start.5 = (bf16[1,1,16,3,8192]{4,2,3,1,0:T(8,128)(2,1)S(1)}, bf16[1,1,16,3,8192]{4,2,3,1,0:T(8,128)(2,1)S(1)}, u32[]{:S(2)}, u32[]{:S(2)}) collective-permute-start(bf16[1,1,16,3,8192]{4,2,3,1,0:T(8,128)(2,1)S(1)} %collective-permute-done.4), channel_id=1, source_target_pairs={{0,16},{16,32},{32,48},{48,64},{64,80},{80,96},{96,112},{112,128},... | collective-permute-start | bytes 2359304 | tf_op jit(solution)/shard_map/ppermute | solution.py:16
  256.2 17.7 %collective-permute-start.12 = (bf16[1,1,16,3,8192]{4,2,3,1,0:T(8,128)(2,1)S(1)}, bf16[1,1,16,3,8192]{4,2,3,1,0:T(8,128)(2,1)}, u32[]{:S(2)}, u32[]{:S(2)}) collective-permute-start(bf16[1,1,16,3,8192]{4,2,3,1,0:T(8,128)(2,1)S(1)} %collective-permute-done.11), channel_id=1, source_target_pairs={{0,240},{16,0},{32,16},{48,32},{64,48},{80,64},{96,80},{112,96},{1... | collective-permute-start | bytes 2359304 | tf_op jit(solution)/shard_map/ppermute | solution.py:18
  273.9 17.8 %collective-permute-start.6 = (bf16[1,1,16,3,8192]{4,2,3,1,0:T(8,128)(2,1)S(1)}, bf16[1,1,16,3,8192]{4,2,3,1,0:T(8,128)(2,1)}, u32[]{:S(2)}, u32[]{:S(2)}) collective-permute-start(bf16[1,1,16,3,8192]{4,2,3,1,0:T(8,128)(2,1)S(1)} %collective-permute-done.5), channel_id=1, source_target_pairs={{0,16},{16,32},{32,48},{48,64},{64,80},{80,96},{96,112},{112,128},... | collective-permute-start | bytes 2359304 | tf_op jit(solution)/shard_map/ppermute | solution.py:16
  273.9 17.8 %collective-permute-start.13 = (bf16[1,1,16,3,8192]{4,2,3,1,0:T(8,128)(2,1)}, bf16[1,1,16,3,8192]{4,2,3,1,0:T(8,128)(2,1)}, u32[]{:S(2)}, u32[]{:S(2)}) collective-permute-start(bf16[1,1,16,3,8192]{4,2,3,1,0:T(8,128)(2,1)} %collective-permute-done.12), channel_id=1, source_target_pairs={{0,240},{16,0},{32,16},{48,32},{64,48},{80,64},{96,80},{112,96},{1... | collective-permute-start | bytes 2359304 | tf_op jit(solution)/shard_map/ppermute | solution.py:18
  291.7 17.1 %collective-permute-start.7 = (bf16[1,1,16,3,8192]{4,2,3,1,0:T(8,128)(2,1)}, bf16[1,1,16,3,8192]{4,2,3,1,0:T(8,128)(2,1)}, u32[]{:S(2)}, u32[]{:S(2)}) collective-permute-start(bf16[1,1,16,3,8192]{4,2,3,1,0:T(8,128)(2,1)} %collective-permute-done.6), channel_id=1, source_target_pairs={{0,16},{16,32},{32,48},{48,64},{64,80},{80,96},{96,112},{112,128},... | collective-permute-start | bytes 2359304 | tf_op jit(solution)/shard_map/ppermute | solution.py:16
  291.7 65.4 %copy-start.20 = (bf16[1,1,16,3,8192]{4,2,3,1,0:T(8,128)(2,1)S(1)}, bf16[1,1,16,3,8192]{4,2,3,1,0:T(8,128)(2,1)}, u32[]{:S(2)}) copy-start(bf16[1,1,16,3,8192]{4,2,3,1,0:T(8,128)(2,1)} %copy-done.19) | copy-start | bytes 2359300
  291.7 67.0 %copy-start.18 = (bf16[1,1,16,3,8192]{4,2,3,1,0:T(8,128)(2,1)S(1)}, bf16[1,1,16,3,8192]{4,2,3,1,0:T(8,128)(2,1)}, u32[]{:S(2)}) copy-start(bf16[1,1,16,3,8192]{4,2,3,1,0:T(8,128)(2,1)} %copy-done.17) | copy-start | bytes 2359300
  291.7 68.7 %copy-start.16 = (bf16[1,1,16,3,8192]{4,2,3,1,0:T(8,128)(2,1)S(1)}, bf16[1,1,16,3,8192]{4,2,3,1,0:T(8,128)(2,1)}, u32[]{:S(2)}) copy-start(bf16[1,1,16,3,8192]{4,2,3,1,0:T(8,128)(2,1)} %copy-done.15) | copy-start | bytes 2359300
  291.7 70.4 %copy-start.10 = (bf16[1,1,16,3,8192]{4,2,3,1,0:T(8,128)(2,1)S(1)}, bf16[1,1,16,3,8192]{4,2,3,1,0:T(8,128)(2,1)}, u32[]{:S(2)}) copy-start(bf16[1,1,16,3,8192]{4,2,3,1,0:T(8,128)(2,1)} %copy-done.9) | copy-start | bytes 2359300
  291.7 72.0 %copy-start.6 = (bf16[1,1,16,3,8192]{4,2,3,1,0:T(8,128)(2,1)S(1)}, bf16[1,1,16,3,8192]{4,2,3,1,0:T(8,128)(2,1)}, u32[]{:S(2)}) copy-start(bf16[1,1,16,3,8192]{4,2,3,1,0:T(8,128)(2,1)} %copy-done.5) | copy-start | bytes 2359300
  291.7 73.7 %copy-start.2 = (bf16[1,1,16,3,8192]{4,2,3,1,0:T(8,128)(2,1)S(1)}, bf16[1,1,16,3,8192]{4,2,3,1,0:T(8,128)(2,1)}, u32[]{:S(2)}) copy-start(bf16[1,1,16,3,8192]{4,2,3,1,0:T(8,128)(2,1)} %copy-done.1) | copy-start | bytes 2359300
  291.7 76.9 %copy-start.4 = (bf16[1,1,16,3,8192]{4,2,3,1,0:T(8,128)(2,1)S(1)}, bf16[1,1,16,3,8192]{4,2,3,1,0:T(8,128)(2,1)}, u32[]{:S(2)}) copy-start(bf16[1,1,16,3,8192]{4,2,3,1,0:T(8,128)(2,1)} %copy-done.3) | copy-start | bytes 2359300
  291.7 78.5 %copy-start.8 = (bf16[1,1,16,3,8192]{4,2,3,1,0:T(8,128)(2,1)S(1)}, bf16[1,1,16,3,8192]{4,2,3,1,0:T(8,128)(2,1)}, u32[]{:S(2)}) copy-start(bf16[1,1,16,3,8192]{4,2,3,1,0:T(8,128)(2,1)} %copy-done.7) | copy-start | bytes 2359300
  291.7 80.2 %copy-start.12 = (bf16[1,1,16,3,8192]{4,2,3,1,0:T(8,128)(2,1)S(1)}, bf16[1,1,16,3,8192]{4,2,3,1,0:T(8,128)(2,1)}, u32[]{:S(2)}) copy-start(bf16[1,1,16,3,8192]{4,2,3,1,0:T(8,128)(2,1)} %copy-done.11) | copy-start | bytes 2359300
  291.8 81.9 %copy-start.14 = (bf16[1,1,16,3,8192]{4,2,3,1,0:T(8,128)(2,1)S(1)}, bf16[1,1,16,3,8192]{4,2,3,1,0:T(8,128)(2,1)}, u32[]{:S(2)}) copy-start(bf16[1,1,16,3,8192]{4,2,3,1,0:T(8,128)(2,1)} %copy-done.13) | copy-start | bytes 2359300
  291.8 57.7 %collective-permute-start.14 = (bf16[1,1,16,3,8192]{4,2,3,1,0:T(8,128)(2,1)}, bf16[1,1,16,3,8192]{4,2,3,1,0:T(8,128)(2,1)S(1)}, u32[]{:S(2)}, u32[]{:S(2)}) collective-permute-start(bf16[1,1,16,3,8192]{4,2,3,1,0:T(8,128)(2,1)} %collective-permute-done.13), channel_id=1, source_target_pairs={{0,240},{16,0},{32,16},{48,32},{64,48},{80,64},{96,80},{112,96},{1... | collective-permute-start | bytes 2359304 | tf_op jit(solution)/shard_map/ppermute | solution.py:18
  420.9 129.0 %copy-start.21 = (s32[16,2]{0,1:T(2,128)S(1)}, s32[16,2]{0,1:T(2,128)}, u32[]{:S(2)}) copy-start(s32[16,2]{0,1:T(2,128)} %param.29) | copy-start | bytes 388
  420.9 129.2 %copy-start.22 = (f32[16,2]{0,1:T(2,128)S(1)}, f32[16,2]{0,1:T(2,128)}, u32[]{:S(2)}) copy-start(f32[16,2]{0,1:T(2,128)} %param.30) | copy-start | bytes 388
  542.0 35.9 %all-to-all-start.2 = ((bf16[1,1,16,3,8192]{4,3,1,0,2:T(4,128)(2,1)}), bf16[1,1,16,3,8192]{4,3,1,0,2:T(4,128)(2,1)}, u32[]{:S(2)}, u32[]{:S(2)}) async-start(bf16[1,1,16,3,8192]{4,3,1,0,2:T(4,128)(2,1)} %copy.122), calls=%async_computation.2 | async-start | bytes 2097152 | tf_op jit(solution)/shard_map/all_to_all | solution.py:143
  (10 other events, 135.6 us)
Sparse Core Ops, SparseCore 0:
  14.1 52.8 all-gather.3
  443.1 96.0 reduce-scatter.6
